TPU v7x, 32 devices: a whole 2x2x4 slice. The times are simulated.
32 devices in a mesh: dp: 2 (over y), tm: 8 (over z, x), height: 2 (over core).
Axes of the slice: x: 2, y: 2, z: 4, core: 2. Of those that a mesh axis runs over, the one named last changes fastest.
Arguments:
- queries: bfloat16 [2, 16, 16, 8, 1536], P('dp', 'tm', 'height'), may hold values from -6 to 6
- keys: bfloat16 [2, 16, 16, 8, 1536], P('dp', 'tm', 'height'), may hold values from -6 to 6
- values: bfloat16 [2, 16, 16, 8, 1536], P('dp', 'tm', 'height'), may hold values from -6 to 6
- text_keys: bfloat16 [2, 256, 1536], P('dp'), may hold values from -110 to 110
- text_values: bfloat16 [2, 256, 1536], P('dp'), may hold values from -6 to 6
- gain_q: float32 [128], replicated, may hold values from 0.5 to 1.5
- gain_k: float32 [128], replicated, may hold values from 0.5 to 1.5
- window_ext: int32 [12, 3], replicated, may hold values from 0 to 1, as said below
- text_len: int32 [2], P('dp'), may hold values from 64 to 256, as said below
- out_grad: bfloat16 [2, 16, 16, 8, 1536], P('dp', 'tm', 'height'), may hold values from -60 to 60
Outputs:
- query_grad: bfloat16 [2, 16, 16, 8, 1536], P('dp', 'tm', 'height')
- key_grad: bfloat16 [2, 16, 16, 8, 1536], P('dp', 'tm', 'height')
- value_grad: bfloat16 [2, 16, 16, 8, 1536], P('dp', 'tm', 'height')
- text_key_grad: float32 [2, 256, 1536], P('dp')
- text_value_grad: float32 [2, 256, 1536], P('dp')
- gain_grads: float32 [2, 128], replicated
Inputs may be any that keep to these rules, and one draw needn't show every extreme that they name: `window_ext`: along each of the three axes some head has reach 1. `text_len`: some sample has all 256 text tokens live.
All inputs are finite; a program needn't handle non-finite values.
Results may differ from a plain program's by a relative error of at most 0.0055.
The roundings to bfloat16 on the way count: a program that leaves them out, or rounds other values in their place, can miss the bound.
Values may be sent and summed in bfloat16 or wider, within the bound.
No kernel may reach another device: no remote copies, remote signals or barrier semaphores. Data moves between devices by JAX's collectives and lax.ppermute only.
A program may use at most 128 MiB of HBM per device.

v0:
```python
import jax
import jax.numpy as jnp
from jax import lax
from jax.sharding import PartitionSpec as P

TILE_F = 2
TILE_H = 4
TILE_W = 4
EPS = 1e-06


def extended(x, sides, width):
    for axis, dim in sides:
        peers, length = (lax.axis_size(axis), x.shape[dim])
        up = [(i, (i + 1) % peers) for i in range(peers - 1)]
        down = [(j, i) for i, j in up]
        last = lax.slice_in_dim(x, length - width, length, axis=dim)
        first = lax.slice_in_dim(x, 0, width, axis=dim)
        before = lax.ppermute(last, axis, up)
        after = lax.ppermute(first, axis, down)
        x = jnp.concatenate([before, x, after], axis=dim)
    return x


def normalize(raw_values, gain_vector, head_count):
    full_shape = raw_values.shape
    head_size = gain_vector.shape[0]
    split_values = raw_values.astype(jnp.float32).reshape(full_shape[:-1] + (head_count, head_size))
    inverse = lax.rsqrt(jnp.mean(split_values * split_values, axis=-1, keepdims=True) + EPS)
    scaled = (split_values * inverse * gain_vector).reshape(full_shape).astype(jnp.bfloat16)
    return (scaled, split_values, inverse)


def norm_backward(grad_out, split_values, inverse, gain_vector):
    full_shape = grad_out.shape
    grad_split = grad_out.reshape(split_values.shape)
    weighted = grad_split * gain_vector
    inner_mean = jnp.mean(weighted * split_values, axis=-1, keepdims=True)
    grad_in = inverse * weighted - split_values * (inverse * inverse * inverse) * inner_mean
    gain_term = jnp.sum(
        (grad_split * split_values * inverse).reshape(-1, gain_vector.shape[0]), axis=0
    )
    return (grad_in.reshape(full_shape), gain_term)


def head_grads(query_head, key_head, value_head, grad_head, allowed):
    score_scale = query_head.shape[-1] ** (-0.5)
    scores = jnp.dot(query_head, key_head.T, preferred_element_type=jnp.float32) * score_scale
    scores = jnp.where(allowed, scores, -1e30)
    peak_score = jnp.max(scores, axis=-1, keepdims=True)
    weights = jnp.exp(scores - peak_score)
    weights = weights / jnp.sum(weights, axis=-1, keepdims=True)
    weights_low = weights.astype(jnp.bfloat16)
    output = jnp.dot(weights_low, value_head, preferred_element_type=jnp.float32)
    delta_row = jnp.sum(grad_head.astype(jnp.float32) * output, axis=-1, keepdims=True)
    value_part = jnp.dot(weights_low.T, grad_head, preferred_element_type=jnp.float32)
    prob_grad = jnp.dot(grad_head, value_head.T, preferred_element_type=jnp.float32)
    score_grad = (weights * (prob_grad - delta_row)).astype(jnp.bfloat16)
    query_part = jnp.dot(score_grad, key_head, preferred_element_type=jnp.float32) * score_scale
    key_part = jnp.dot(score_grad.T, query_head, preferred_element_type=jnp.float32) * score_scale
    return (query_part, key_part, value_part)


def split_heads(matrix, head_count):
    return matrix.reshape(matrix.shape[0], head_count, -1).transpose(1, 0, 2)


def merge_heads(stacked):
    return stacked.transpose(1, 0, 2).reshape(stacked.shape[1], -1)


def tile_window(first_tiles, second_tiles, extent):
    within = jnp.abs(first_tiles[:, None, 0] - second_tiles[None, :, 0]) <= extent[0]
    within = within & (jnp.abs(first_tiles[:, None, 1] - second_tiles[None, :, 1]) <= extent[1])
    return within & (jnp.abs(first_tiles[:, None, 2] - second_tiles[None, :, 2]) <= extent[2])


def allowed_mask(query_tiles, key_tiles, key_valid, text_valid, extent):
    within = tile_window(query_tiles, key_tiles, extent)
    video_mask = within & key_valid[None, :]
    text_mask = jnp.broadcast_to(text_valid[None, :], (query_tiles.shape[0], text_valid.shape[0]))
    return jnp.concatenate([video_mask, text_mask], axis=1)


def attend_all(
    query_flat,
    key_flat,
    value_flat,
    grad_flat,
    extents,
    query_tiles,
    key_tiles,
    key_valid,
    text_valid,
):
    head_count = extents.shape[0]

    def per_head(operands):
        query_head, key_head, value_head, grad_head, extent = operands
        allowed = allowed_mask(query_tiles, key_tiles, key_valid, text_valid, extent)
        return head_grads(query_head, key_head, value_head, grad_head, allowed)

    grad_query, grad_keys, grad_values = lax.map(
        per_head,
        (
            split_heads(query_flat, head_count),
            split_heads(key_flat, head_count),
            split_heads(value_flat, head_count),
            split_heads(grad_flat, head_count),
            extents,
        ),
    )
    return (merge_heads(grad_query), merge_heads(grad_keys), merge_heads(grad_values))


def tile_coords(frame_index, row_index, column_index):
    full_shape = (frame_index.shape[0], row_index.shape[0], column_index.shape[0])
    pieces = [
        jnp.broadcast_to((frame_index // TILE_F)[:, None, None], full_shape),
        jnp.broadcast_to((row_index // TILE_H)[None, :, None], full_shape),
        jnp.broadcast_to((column_index // TILE_W)[None, None, :], full_shape),
    ]
    return jnp.stack(pieces, axis=-1).reshape(-1, 3)


def fold_axis(array, axis_number, width, inner_count):
    owned = lax.slice_in_dim(array, 2 * width, 2 * width + inner_count, axis=axis_number)
    lower = lax.slice_in_dim(array, 0, width, axis=axis_number)
    upper = lax.slice_in_dim(
        array, inner_count + 3 * width, inner_count + 4 * width, axis=axis_number
    )
    low_pad = [(0, 0)] * array.ndim
    high_pad = [(0, 0)] * array.ndim
    low_pad[axis_number] = (0, inner_count - width)
    high_pad[axis_number] = (inner_count - width, 0)
    return owned + jnp.pad(lower, low_pad) + jnp.pad(upper, high_pad)


def local(
    queries, keys, values, text_keys, text_values, gain_q, gain_k, window_ext, text_len, out_grad
):
    head_count = window_ext.shape[0]
    frame_count, row_count, column_count, feature_count = queries.shape[1:]
    text_count = text_keys.shape[1]
    frame_base = lax.axis_index("tm") * frame_count
    row_base = lax.axis_index("height") * row_count
    total_frames = frame_count * lax.axis_size("tm")
    total_rows = row_count * lax.axis_size("height")
    query_norm, query_split, query_inverse = normalize(queries[0], gain_q, head_count)
    key_norm, key_split, key_inverse = normalize(keys[0], gain_k, head_count)
    stacked = jnp.stack([key_norm, values[0]])
    rowed = extended(stacked, (("height", 2),), TILE_H)
    beside_all = extended(rowed, (("tm", 1),), TILE_F)
    frames_wide = frame_count + 2 * TILE_F
    rows_wide = row_count + 2 * TILE_H
    column_index = jnp.arange(column_count)
    query_frames = frame_base + jnp.arange(frame_count)
    query_rows = row_base + jnp.arange(row_count)
    key_frames = frame_base - TILE_F + jnp.arange(frames_wide)
    key_rows = row_base - TILE_H + jnp.arange(rows_wide)
    query_tiles = tile_coords(query_frames, query_rows, column_index)
    key_tiles = tile_coords(key_frames, key_rows, column_index)
    frame_valid = (key_frames >= 0) & (key_frames < total_frames)
    row_valid = (key_rows >= 0) & (key_rows < total_rows)
    key_valid = jnp.broadcast_to(
        frame_valid[:, None, None] & row_valid[None, :, None],
        (frames_wide, rows_wide, column_count),
    ).reshape(-1)
    text_valid = jnp.arange(text_count) < text_len[0]
    key_all = jnp.concatenate([beside_all[0].reshape(-1, feature_count), text_keys[0]], axis=0)
    value_all = jnp.concatenate([beside_all[1].reshape(-1, feature_count), text_values[0]], axis=0)
    query_flat = query_norm.reshape(-1, feature_count)
    grad_flat = out_grad[0].reshape(-1, feature_count)
    video_count = frames_wide * rows_wide * column_count
    grad_query, grad_keys, grad_values = attend_all(
        query_flat,
        key_all,
        value_all,
        grad_flat,
        window_ext,
        query_tiles,
        key_tiles,
        key_valid,
        text_valid,
    )
    grads = jnp.stack([grad_keys[:video_count], grad_values[:video_count]]).reshape(
        2, frames_wide, rows_wide, column_count, feature_count
    )
    returned = extended(grads, (("tm", 1),), TILE_F)
    partial_sum = fold_axis(returned, 1, TILE_F, frame_count)
    returned_rows = extended(partial_sum, (("height", 2),), TILE_H)
    owned = fold_axis(returned_rows, 2, TILE_H, row_count)
    key_own = owned[0]
    value_own = owned[1]
    text_key_part = grad_keys[video_count:]
    text_value_part = grad_values[video_count:]
    query_full = grad_query.reshape(frame_count, row_count, column_count, feature_count)
    query_out, query_gain = norm_backward(query_full, query_split, query_inverse, gain_q)
    key_out, key_gain = norm_backward(key_own, key_split, key_inverse, gain_k)
    gain_terms = jnp.stack([query_gain, key_gain])
    text_key_sum, text_value_sum = lax.psum((text_key_part, text_value_part), ("tm", "height"))
    gain_total = lax.psum(gain_terms, ("dp", "tm", "height"))
    return (
        query_out.astype(jnp.bfloat16)[None],
        key_out.astype(jnp.bfloat16)[None],
        value_own.astype(jnp.bfloat16)[None],
        text_key_sum[None],
        text_value_sum[None],
        gain_total,
    )


def solution(mesh):
    return jax.shard_map(
        local,
        mesh=mesh,
        in_specs=(
            P("dp", "tm", "height", None, None),
            P("dp", "tm", "height", None, None),
            P("dp", "tm", "height", None, None),
            P("dp", None, None),
            P("dp", None, None),
            P(),
            P(),
            P(),
            P("dp"),
            P("dp", "tm", "height", None, None),
        ),
        out_specs=(
            P("dp", "tm", "height", None, None),
            P("dp", "tm", "height", None, None),
            P("dp", "tm", "height", None, None),
            P("dp", None, None),
            P("dp", None, None),
            P(),
        ),
        check_vma=False,
    )
```

profile of v0, /device:TPU:0, one launch (start us, length us, event | category | flops | bytes accessed | tf_op | source)
XLA Modules:
  0.0 574.4 jit_solution(11806287769408357860)
XLA Ops:
  12.3 2.4 collective-permute-start
  21.0 6.0 %collective-permute-start.2 = (bf16[2,2,16,8,1536]{4,3,2,1,0:T(8,128)(2,1)}, bf16[2,2,16,8,1536]{4,3,2,1,0:T(8,128)(2,1)}, u32[]{:S(2)}, u32[]{:S(2)}) collective-permute-start(bf16[2,2,16,8,1536]{4,3,2,1,0:T(8,128)(2,1)} %pad_maximum_fusion.1), channel_id=1, source_target_pairs={{0,2},{2,4},{4,6},{6,8},{8,10},{10,12},{12,14},{1,3},{3,5},{5,7},{... | collective-permute-start | bytes 4718600 | tf_op jit(solution)/shard_map/ppermute | solution.py:19
  40.6 18.4 %collective-permute-done.3 = bf16[2,2,16,8,1536]{4,3,2,1,0:T(8,128)(2,1)} collective-permute-done((bf16[2,2,16,8,1536]{4,3,2,1,0:T(8,128)(2,1)}, bf16[2,2,16,8,1536]{4,3,2,1,0:T(8,128)(2,1)}, u32[]{:S(2)}, u32[]{:S(2)}) %collective-permute-start.3) | collective-permute-done | bytes 1572896 | tf_op jit(solution)/shard_map/ppermute | solution.py:20
  59.0 33.9 %collective-permute-done.2 = bf16[2,2,16,8,1536]{4,3,2,1,0:T(8,128)(2,1)} collective-permute-done((bf16[2,2,16,8,1536]{4,3,2,1,0:T(8,128)(2,1)}, bf16[2,2,16,8,1536]{4,3,2,1,0:T(8,128)(2,1)}, u32[]{:S(2)}, u32[]{:S(2)}) %collective-permute-start.2) | collective-permute-done | bytes 1572896 | tf_op jit(solution)/shard_map/ppermute | solution.py:19
  92.8 3.0 pad_maximum_fusion
  95.8 2.8 fusion.59
  98.6 4.2 concatenate.31
  104.6 2.4 copy.80
  107.1 4.2 concatenate.28
  113.2 2.5 copy.78
  115.7 173.7 %while.15 = (s32[]{:T(128)}, f32[12,128,128]{2,0,1:T(8,128)S(1)}, f32[12,1024,128]{1,2,0:T(8,128)}, f32[12,1024,128]{1,2,0:T(8,128)}, s32[128,3]{0,1:T(4,128)S(1...) while((s32[]{:T(128)}, f32[12,128,128]{2,0,1:T(8,128)S(1)}, ...), condition=%wide.region_6.7_spmd.clone, body=%wide.region_2.6_spmd.clone.sunk | while | flops 204930944 | bytes 8207186 | solution.py:103
  117.2 2.3 fusion.92
  131.7 2.3 fusion.92
  146.2 2.3 fusion.92
  160.6 2.3 fusion.92
  289.4 5.2 slice.118
  294.5 6.6 %copy.85 = f32[768,12,128]{2,1,0:T(8,128)} copy(f32[768,12,128]{0,2,1:T(8,128)} %slice.118) | data formatting | bytes 9437184 | tf_op jit(solution)/shard_map/slice | solution.py:186
  301.2 6.8 %stack.31 = f32[1,6,16,8,1536]{4,3,2,1,0:T(8,128)} reshape(f32[768,12,128]{2,1,0:T(8,128)} %copy.85) | data formatting | bytes 9437184 | tf_op jit(solution)/shard_map/stack | solution.py:186
  307.9 4.9 slice.119
  312.8 6.6 %copy.87 = f32[768,12,128]{2,1,0:T(8,128)} copy(f32[768,12,128]{0,2,1:T(8,128)} %slice.119) | data formatting | bytes 9437184 | tf_op jit(solution)/shard_map/slice | solution.py:186
  319.4 6.8 %stack.32 = f32[1,6,16,8,1536]{4,3,2,1,0:T(8,128)} reshape(f32[768,12,128]{2,1,0:T(8,128)} %copy.87) | data formatting | bytes 9437184 | tf_op jit(solution)/shard_map/stack | solution.py:186
  326.1 2.8 constant_dynamic-update-slice_fusion.2
  330.2 3.4 fusion.58
  335.8 4.8 collective-permute-start.4
  345.2 2.7 slice.128
  347.9 2.7 slice.129
  350.6 141.3 %collective-permute-done.4 = f32[2,2,16,8,1536]{4,3,2,1,0:T(8,128)S(1)} collective-permute-done((f32[2,2,16,8,1536]{4,3,2,1,0:T(8,128)}, f32[2,2,16,8,1536]{4,3,2,1,0:T(8,128)S(1)}, u32[]{:S(2)}, u32[]{:S(2)}) %collective-permute-start.4) | collective-permute-done | bytes 3145760 | tf_op jit(solution)/shard_map/ppermute | solution.py:19
  493.5 4.8 fusion.41
  512.6 2.6 fusion.53
  515.2 3.0 copy.89
  518.3 3.0 copy.90
  526.0 41.6 %psum.23 = f32[2,128]{1,0:T(2,128)} all-reduce(f32[2,128]{1,0:T(2,128)S(1)} %pad_maximum_fusion.3), channel_id=1, replica_groups=mesh['dp'=2,'tm'=8,'height'=2] {'dp','tm','height'}, use_global_device_ids=true, to_apply=%region_13.14 | all-reduce | flops 256 | bytes 2048 | tf_op jit(solution)/shard_map/psum | solution.py:202
  (349 shorter events, 220.7 us)
Async XLA Ops:
  7.2 11.2 %copy-start.8 = (bf16[1,2,8,8,1536]{4,3,2,1,0:T(8,128)(2,1)S(1)}, bf16[1,2,8,8,1536]{4,3,2,1,0:T(8,128)(2,1)}, u32[]{:S(2)}) copy-start(bf16[1,2,8,8,1536]{4,3,2,1,0:T(8,128)(2,1)} %param.14) | copy-start | bytes 1179652
  7.2 508.1 %all-reduce.5.cloned.1.call-start = ((), (), s32[]{:S(2)}) async-start(), calls=%async_computation | async-start | bytes 6291456 | tf_op jit(solution)/shard_map/psum | solution.py:201
  7.9 6.9 %copy-start.18 = (f32[1536]{0:T(1024)}, f32[1536]{0:T(1024)S(1)}, u32[]{:S(2)}) copy-start(f32[1536]{0:T(1024)S(1)} %broadcast_bitcast_fusion.1) | copy-start | bytes 18436
  9.9 17.8 %copy-start.11 = (f32[2,8,8,12]{2,3,1,0:T(8,128)}, f32[2,8,8,12]{2,3,1,0:T(8,128)S(1)}, u32[]{:S(2)}) copy-start(f32[2,8,8,12]{2,3,1,0:T(8,128)S(1)} %get-tuple-element.218) | copy-start | bytes 18436
  9.9 17.8 %copy-start.9 = (bf16[1,2,8,8,1536]{4,3,2,1,0:T(8,128)(2,1)S(1)}, bf16[1,2,8,8,1536]{4,3,2,1,0:T(8,128)(2,1)}, u32[]{:S(2)}) copy-start(bf16[1,2,8,8,1536]{4,3,2,1,0:T(8,128)(2,1)} %param.12) | copy-start | bytes 1179652
  12.3 3.8 collective-permute-start
  14.8 3.6 collective-permute-start.1
  18.4 10.6 %copy-start.13 = (bf16[2,2,4,8,1536]{4,3,2,1,0:T(8,128)(2,1)}, bf16[2,2,4,8,1536]{4,3,2,1,0:T(8,128)(2,1)S(1)}, u32[]{:S(2)}) copy-start(bf16[2,2,4,8,1536]{4,3,2,1,0:T(8,128)(2,1)S(1)} %collective-permute-done.1) | copy-start | bytes 1179652
  19.7 39.2 %collective-permute-start.3 = (bf16[2,2,16,8,1536]{4,3,2,1,0:T(8,128)(2,1)}, bf16[2,2,16,8,1536]{4,3,2,1,0:T(8,128)(2,1)}, u32[]{:S(2)}, u32[]{:S(2)}) collective-permute-start(bf16[2,2,16,8,1536]{4,3,2,1,0:T(8,128)(2,1)} %pad_maximum_fusion.1), channel_id=1, source_target_pairs={{2,0},{4,2},{6,4},{8,6},{10,8},{12,10},{14,12},{3,1},{5,3},{7,5},{... | collective-permute-start | bytes 4718600 | tf_op jit(solution)/shard_map/ppermute | solution.py:20
  21.0 71.8 %collective-permute-start.2 = (bf16[2,2,16,8,1536]{4,3,2,1,0:T(8,128)(2,1)}, bf16[2,2,16,8,1536]{4,3,2,1,0:T(8,128)(2,1)}, u32[]{:S(2)}, u32[]{:S(2)}) collective-permute-start(bf16[2,2,16,8,1536]{4,3,2,1,0:T(8,128)(2,1)} %pad_maximum_fusion.1), channel_id=1, source_target_pairs={{0,2},{2,4},{4,6},{6,8},{8,10},{10,12},{12,14},{1,3},{3,5},{5,7},{... | collective-permute-start | bytes 4718600 | tf_op jit(solution)/shard_map/ppermute | solution.py:19
  27.9 10.8 %copy-start.2 = (f32[128,12,128]{2,1,0:T(8,128)}, f32[128,12,128]{2,1,0:T(8,128)S(1)}, u32[]{:S(2)}) copy-start(f32[128,12,128]{2,1,0:T(8,128)S(1)} %reshape.281) | copy-start | bytes 2359300
  29.8 8.9 %copy-start.15 = (f32[2,8,8,12]{3,2,1,0:T(8,128)}, f32[2,8,8,12]{3,2,1,0:T(8,128)S(1)}, u32[]{:S(2)}) copy-start(f32[2,8,8,12]{3,2,1,0:T(8,128)S(1)} %copy.91) | copy-start | bytes 18436
  32.2 6.5 %copy-start.22 = (f32[128]{0:T(128)S(1)}, f32[128]{0:T(128)}, u32[]{:S(2)}) copy-start(f32[128]{0:T(128)} %param.17) | copy-start | bytes 1540
  113.2 2.5 copy-start.5
  113.2 2.5 copy-start.20
  113.2 2.5 copy-start.21
  289.4 5.2 copy-start.6
  326.1 3.8 copy-start.1
  330.2 5.6 copy-start
  335.8 156.0 %collective-permute-start.4 = (f32[2,2,16,8,1536]{4,3,2,1,0:T(8,128)}, f32[2,2,16,8,1536]{4,3,2,1,0:T(8,128)S(1)}, u32[]{:S(2)}, u32[]{:S(2)}) collective-permute-start(f32[2,2,16,8,1536]{4,3,2,1,0:T(8,128)} %get-tuple-element.207), channel_id=1, source_target_pairs={{0,2},{2,4},{4,6},{6,8},{8,10},{10,12},{12,14},{1,3},{3,5},{5,7},{... | collective-permute-start | bytes 9437192 | tf_op jit(solution)/shard_map/ppermute | solution.py:19
  340.7 152.9 %collective-permute-start.5 = (f32[2,2,16,8,1536]{4,3,2,1,0:T(8,128)}, f32[2,2,16,8,1536]{4,3,2,1,0:T(8,128)}, u32[]{:S(2)}, u32[]{:S(2)}) collective-permute-start(f32[2,2,16,8,1536]{4,3,2,1,0:T(8,128)} %get-tuple-element.208), channel_id=1, source_target_pairs={{2,0},{4,2},{6,4},{8,6},{10,8},{12,10},{14,12},{3,1},{5,3},{7,5},{... | collective-permute-start | bytes 9437192 | tf_op jit(solution)/shard_map/ppermute | solution.py:20
  498.4 4.8 copy-start.3
  498.4 4.8 copy-start.7
  498.4 4.8 copy-start.16
  498.4 4.8 copy-start.23
  499.7 21.6 %collective-permute-start.6 = (f32[2,2,4,8,1536]{4,3,2,1,0:T(8,128)}, f32[2,2,4,8,1536]{4,3,2,1,0:T(8,128)}, u32[]{:S(2)}, u32[]{:S(2)}) collective-permute-start(f32[2,2,4,8,1536]{4,3,2,1,0:T(8,128)} %get-tuple-element.211), channel_id=1, source_target_pairs={{0,1},{2,3},{4,5},{6,7},{8,9},{10,11},{12,13},{14,15},{16,17},{18,... | collective-permute-start | bytes 2359304 | tf_op jit(solution)/shard_map/ppermute | solution.py:19
  501.9 19.4 %collective-permute-start.7 = (f32[2,2,4,8,1536]{4,3,2,1,0:T(8,128)}, f32[2,2,4,8,1536]{4,3,2,1,0:T(8,128)}, u32[]{:S(2)}, u32[]{:S(2)}) collective-permute-start(f32[2,2,4,8,1536]{4,3,2,1,0:T(8,128)} %get-tuple-element.212), channel_id=1, source_target_pairs={{1,0},{3,2},{5,4},{7,6},{9,8},{11,10},{13,12},{15,14},{17,16},{19,... | collective-permute-start | bytes 2359304 | tf_op jit(solution)/shard_map/ppermute | solution.py:20
  521.3 1.7 copy-start.24
  521.3 2.8 copy-start.12
  521.3 2.8 copy-start.17
  521.3 2.8 copy-start.19
  523.3 2.7 copy-start.25
  (3 other events, 4.0 us)
Sparse Core Ops, SparseCore 0:
  350.7 164.4 all-reduce.4
where the time goes:
time: 579 us; the launch traced here: 574 us
  waiting for transfers between devices  196 us (34%)
  local copies, waits for them, and re-layouts  139 us (24%)
  matrix products  95.2 us (16%)
  other arithmetic  66.2 us (11%)
  blocking collectives  41.6 us (7%)
  starting transfers between devices  20.6 us (4%)
  between operations  14.5 us (3%)
    ppermute x4, waiting for transfers between devices, extended(): before = lax.ppermute(last, axis, up)  175 us
    psum x1, blocking collectives, local(): gain_total = lax.psum(gain_terms, ('dp', 'tm', 'height'))  41.6 us
    dynamic_update_slice x36, local copies, waits for them, and re-layouts, attend_all(): lax.map(per_head, (split_heads(query_flat, head_count), split_heads(key_f...  29.8 us
    and x12, other arithmetic, allowed_mask(): video_mask = within & key_valid[None, :]  27.4 us
    unnamed x61, local copies, waits for them, and re-layouts  24.1 us
    dot_general x12, matrix products, head_grads(): jnp.dot(weights_low.T, grad_head, preferred_element_type=jnp.float32)  22.7 us
    ppermute x4, waiting for transfers between devices, extended(): after = lax.ppermute(first, axis, down)  20.7 us
    dot_general x12, matrix products, head_grads(): jnp.dot(weights_low, value_head, preferred_element_type=jnp.float32)  15.8 us
  transfers between devices with their start and end apart: 9, of which 5 were waited for; matrix products, arithmetic and copies ran while one was open for 8% of the time, Pallas kernels for 0%

commit v1 on v0

--- a/solution.py
+++ b/solution.py
@@ -199,7 +199,7 @@
     key_out, key_gain = norm_backward(key_own, key_split, key_inverse, gain_k)
     gain_terms = jnp.stack([query_gain, key_gain])
     text_key_sum, text_value_sum = lax.psum((text_key_part, text_value_part), ("tm", "height"))
-    gain_total = lax.psum(gain_terms, ("dp", "tm", "height"))
+    gain_total = jnp.sum(lax.all_gather(gain_terms, ("dp", "tm", "height")), axis=0)
     return (
         query_out.astype(jnp.bfloat16)[None],
         key_out.astype(jnp.bfloat16)[None],

time: 579 us -> 578 us (level)
    psum x1 -> x0, blocking collectives: 41.6 us -> none  [local(): gain_total = lax.psum(gain_terms, ('dp', 'tm', 'height'))]
    all_gather x0 -> x1, blocking collectives: none -> 40 us  [local(): lax.all_gather(gain_terms, ('dp', 'tm', 'height'))]
where the time goes in v1:
time: 578 us; the launch traced here: 573 us
  waiting for transfers between devices  196 us (34%)
  local copies, waits for them, and re-layouts  139 us (24%)
  matrix products  95.2 us (16%)
  other arithmetic  66.8 us (12%)
  blocking collectives  40 us (7%)
  starting transfers between devices  20.6 us (4%)
  between operations  14.5 us (3%)
    ppermute x4, waiting for transfers between devices, extended(): before = lax.ppermute(last, axis, up)  175 us
    all_gather x1, blocking collectives, local(): lax.all_gather(gain_terms, ('dp', 'tm', 'height'))  40 us
    dynamic_update_slice x36, local copies, waits for them, and re-layouts, attend_all(): lax.map(per_head, (split_heads(query_flat, head_count), split_heads(key_f...  29.8 us
    and x12, other arithmetic, allowed_mask(): video_mask = within & key_valid[None, :]  27.4 us
    unnamed x61, local copies, waits for them, and re-layouts  24.1 us
    dot_general x12, matrix products, head_grads(): jnp.dot(weights_low.T, grad_head, preferred_element_type=jnp.float32)  22.7 us
    ppermute x4, waiting for transfers between devices, extended(): after = lax.ppermute(first, axis, down)  20.7 us
    dot_general x12, matrix products, head_grads(): jnp.dot(weights_low, value_head, preferred_element_type=jnp.float32)  15.8 us
  transfers between devices with their start and end apart: 9, of which 5 were waited for; matrix products, arithmetic and copies ran while one was open for 8% of the time, Pallas kernels for 0%

profile of v1, /device:TPU:0, one launch (start us, length us, event | category | flops | bytes accessed | tf_op | source)
XLA Modules:
  0.0 573.4 jit_solution(8663218373155163686)
XLA Ops:
  12.3 2.4 collective-permute-start
  21.0 6.0 %collective-permute-start.2 = (bf16[2,2,16,8,1536]{4,3,2,1,0:T(8,128)(2,1)}, bf16[2,2,16,8,1536]{4,3,2,1,0:T(8,128)(2,1)}, u32[]{:S(2)}, u32[]{:S(2)}) collective-permute-start(bf16[2,2,16,8,1536]{4,3,2,1,0:T(8,128)(2,1)} %pad_maximum_fusion.1), channel_id=1, source_target_pairs={{0,2},{2,4},{4,6},{6,8},{8,10},{10,12},{12,14},{1,3},{3,5},{5,7},{... | collective-permute-start | bytes 4718600 | tf_op jit(solution)/shard_map/ppermute | solution.py:19
  40.6 18.4 %collective-permute-done.3 = bf16[2,2,16,8,1536]{4,3,2,1,0:T(8,128)(2,1)} collective-permute-done((bf16[2,2,16,8,1536]{4,3,2,1,0:T(8,128)(2,1)}, bf16[2,2,16,8,1536]{4,3,2,1,0:T(8,128)(2,1)}, u32[]{:S(2)}, u32[]{:S(2)}) %collective-permute-start.3) | collective-permute-done | bytes 1572896 | tf_op jit(solution)/shard_map/ppermute | solution.py:20
  59.0 33.9 %collective-permute-done.2 = bf16[2,2,16,8,1536]{4,3,2,1,0:T(8,128)(2,1)} collective-permute-done((bf16[2,2,16,8,1536]{4,3,2,1,0:T(8,128)(2,1)}, bf16[2,2,16,8,1536]{4,3,2,1,0:T(8,128)(2,1)}, u32[]{:S(2)}, u32[]{:S(2)}) %collective-permute-start.2) | collective-permute-done | bytes 1572896 | tf_op jit(solution)/shard_map/ppermute | solution.py:19
  92.8 3.0 pad_maximum_fusion
  95.8 2.8 fusion.59
  98.6 4.2 concatenate.31
  104.6 2.4 copy.80
  107.1 4.2 concatenate.28
  113.2 2.5 copy.78
  115.7 173.7 %while.15 = (s32[]{:T(128)}, f32[12,128,128]{2,0,1:T(8,128)S(1)}, f32[12,1024,128]{1,2,0:T(8,128)}, f32[12,1024,128]{1,2,0:T(8,128)}, s32[128,3]{0,1:T(4,128)S(1...) while((s32[]{:T(128)}, f32[12,128,128]{2,0,1:T(8,128)S(1)}, ...), condition=%wide.region_6.7_spmd.clone, body=%wide.region_2.6_spmd.clone.sunk | while | flops 204930944 | bytes 8207186 | solution.py:103
  117.2 2.3 fusion.92
  131.7 2.3 fusion.92
  146.2 2.3 fusion.92
  160.6 2.3 fusion.92
  289.4 5.2 slice.118
  294.5 6.6 %copy.85 = f32[768,12,128]{2,1,0:T(8,128)} copy(f32[768,12,128]{0,2,1:T(8,128)} %slice.118) | data formatting | bytes 9437184 | tf_op jit(solution)/shard_map/slice | solution.py:186
  301.2 6.8 %stack.31 = f32[1,6,16,8,1536]{4,3,2,1,0:T(8,128)} reshape(f32[768,12,128]{2,1,0:T(8,128)} %copy.85) | data formatting | bytes 9437184 | tf_op jit(solution)/shard_map/stack | solution.py:186
  307.9 4.9 slice.119
  312.8 6.6 %copy.87 = f32[768,12,128]{2,1,0:T(8,128)} copy(f32[768,12,128]{0,2,1:T(8,128)} %slice.119) | data formatting | bytes 9437184 | tf_op jit(solution)/shard_map/slice | solution.py:186
  319.4 6.8 %stack.32 = f32[1,6,16,8,1536]{4,3,2,1,0:T(8,128)} reshape(f32[768,12,128]{2,1,0:T(8,128)} %copy.87) | data formatting | bytes 9437184 | tf_op jit(solution)/shard_map/stack | solution.py:186
  326.1 2.8 constant_dynamic-update-slice_fusion.2
  330.2 3.4 fusion.58
  335.8 4.8 collective-permute-start.4
  345.2 2.7 slice.128
  347.9 2.7 slice.129
  350.6 141.3 %collective-permute-done.4 = f32[2,2,16,8,1536]{4,3,2,1,0:T(8,128)S(1)} collective-permute-done((f32[2,2,16,8,1536]{4,3,2,1,0:T(8,128)}, f32[2,2,16,8,1536]{4,3,2,1,0:T(8,128)S(1)}, u32[]{:S(2)}, u32[]{:S(2)}) %collective-permute-start.4) | collective-permute-done | bytes 3145760 | tf_op jit(solution)/shard_map/ppermute | solution.py:19
  493.5 4.8 fusion.41
  512.6 2.6 fusion.53
  515.2 3.0 copy.89
  518.3 3.0 copy.90
  526.0 40.0 %all-gather.1 = f32[32,2,128]{2,1,0:T(2,128)S(1)} all-gather(f32[1,2,128]{2,1,0:T(2,128)S(1)} %maximum_bitcast_fusion.2), channel_id=2, replica_groups=mesh['dp'=2,'tm'=8,'height'=2] {'dp','tm','height'}, dimensions={0}, use_global_device_ids=true | all-gather | bytes 33792 | tf_op jit(solution)/shard_map/all_gather | solution.py:202
  (350 shorter events, 221.3 us)
Async XLA Ops:
  7.2 11.2 %copy-start.8 = (bf16[1,2,8,8,1536]{4,3,2,1,0:T(8,128)(2,1)S(1)}, bf16[1,2,8,8,1536]{4,3,2,1,0:T(8,128)(2,1)}, u32[]{:S(2)}) copy-start(bf16[1,2,8,8,1536]{4,3,2,1,0:T(8,128)(2,1)} %param.14) | copy-start | bytes 1179652
  7.2 508.1 %all-reduce.5.cloned.1.call-start = ((), (), s32[]{:S(2)}) async-start(), calls=%async_computation | async-start | bytes 6291456 | tf_op jit(solution)/shard_map/psum | solution.py:201
  7.9 6.9 %copy-start.18 = (f32[1536]{0:T(1024)}, f32[1536]{0:T(1024)S(1)}, u32[]{:S(2)}) copy-start(f32[1536]{0:T(1024)S(1)} %broadcast_bitcast_fusion.1) | copy-start | bytes 18436
  9.9 17.8 %copy-start.11 = (f32[2,8,8,12]{2,3,1,0:T(8,128)}, f32[2,8,8,12]{2,3,1,0:T(8,128)S(1)}, u32[]{:S(2)}) copy-start(f32[2,8,8,12]{2,3,1,0:T(8,128)S(1)} %get-tuple-element.218) | copy-start | bytes 18436
  9.9 17.8 %copy-start.9 = (bf16[1,2,8,8,1536]{4,3,2,1,0:T(8,128)(2,1)S(1)}, bf16[1,2,8,8,1536]{4,3,2,1,0:T(8,128)(2,1)}, u32[]{:S(2)}) copy-start(bf16[1,2,8,8,1536]{4,3,2,1,0:T(8,128)(2,1)} %param.12) | copy-start | bytes 1179652
  12.3 3.8 collective-permute-start
  14.8 3.6 collective-permute-start.1
  18.4 10.6 %copy-start.13 = (bf16[2,2,4,8,1536]{4,3,2,1,0:T(8,128)(2,1)}, bf16[2,2,4,8,1536]{4,3,2,1,0:T(8,128)(2,1)S(1)}, u32[]{:S(2)}) copy-start(bf16[2,2,4,8,1536]{4,3,2,1,0:T(8,128)(2,1)S(1)} %collective-permute-done.1) | copy-start | bytes 1179652
  19.7 39.2 %collective-permute-start.3 = (bf16[2,2,16,8,1536]{4,3,2,1,0:T(8,128)(2,1)}, bf16[2,2,16,8,1536]{4,3,2,1,0:T(8,128)(2,1)}, u32[]{:S(2)}, u32[]{:S(2)}) collective-permute-start(bf16[2,2,16,8,1536]{4,3,2,1,0:T(8,128)(2,1)} %pad_maximum_fusion.1), channel_id=1, source_target_pairs={{2,0},{4,2},{6,4},{8,6},{10,8},{12,10},{14,12},{3,1},{5,3},{7,5},{... | collective-permute-start | bytes 4718600 | tf_op jit(solution)/shard_map/ppermute | solution.py:20
  21.0 71.8 %collective-permute-start.2 = (bf16[2,2,16,8,1536]{4,3,2,1,0:T(8,128)(2,1)}, bf16[2,2,16,8,1536]{4,3,2,1,0:T(8,128)(2,1)}, u32[]{:S(2)}, u32[]{:S(2)}) collective-permute-start(bf16[2,2,16,8,1536]{4,3,2,1,0:T(8,128)(2,1)} %pad_maximum_fusion.1), channel_id=1, source_target_pairs={{0,2},{2,4},{4,6},{6,8},{8,10},{10,12},{12,14},{1,3},{3,5},{5,7},{... | collective-permute-start | bytes 4718600 | tf_op jit(solution)/shard_map/ppermute | solution.py:19
  27.9 10.8 %copy-start.2 = (f32[128,12,128]{2,1,0:T(8,128)}, f32[128,12,128]{2,1,0:T(8,128)S(1)}, u32[]{:S(2)}) copy-start(f32[128,12,128]{2,1,0:T(8,128)S(1)} %reshape.281) | copy-start | bytes 2359300
  29.8 8.9 %copy-start.15 = (f32[2,8,8,12]{3,2,1,0:T(8,128)}, f32[2,8,8,12]{3,2,1,0:T(8,128)S(1)}, u32[]{:S(2)}) copy-start(f32[2,8,8,12]{3,2,1,0:T(8,128)S(1)} %copy.91) | copy-start | bytes 18436
  32.2 6.5 %copy-start.22 = (f32[128]{0:T(128)S(1)}, f32[128]{0:T(128)}, u32[]{:S(2)}) copy-start(f32[128]{0:T(128)} %param.17) | copy-start | bytes 1540
  113.2 2.5 copy-start.5
  113.2 2.5 copy-start.20
  113.2 2.5 copy-start.21
  289.4 5.2 copy-start.6
  326.1 3.8 copy-start.1
  330.2 5.6 copy-start
  335.8 156.0 %collective-permute-start.4 = (f32[2,2,16,8,1536]{4,3,2,1,0:T(8,128)}, f32[2,2,16,8,1536]{4,3,2,1,0:T(8,128)S(1)}, u32[]{:S(2)}, u32[]{:S(2)}) collective-permute-start(f32[2,2,16,8,1536]{4,3,2,1,0:T(8,128)} %get-tuple-element.207), channel_id=1, source_target_pairs={{0,2},{2,4},{4,6},{6,8},{8,10},{10,12},{12,14},{1,3},{3,5},{5,7},{... | collective-permute-start | bytes 9437192 | tf_op jit(solution)/shard_map/ppermute | solution.py:19
  340.7 152.9 %collective-permute-start.5 = (f32[2,2,16,8,1536]{4,3,2,1,0:T(8,128)}, f32[2,2,16,8,1536]{4,3,2,1,0:T(8,128)}, u32[]{:S(2)}, u32[]{:S(2)}) collective-permute-start(f32[2,2,16,8,1536]{4,3,2,1,0:T(8,128)} %get-tuple-element.208), channel_id=1, source_target_pairs={{2,0},{4,2},{6,4},{8,6},{10,8},{12,10},{14,12},{3,1},{5,3},{7,5},{... | collective-permute-start | bytes 9437192 | tf_op jit(solution)/shard_map/ppermute | solution.py:20
  498.4 4.8 copy-start.3
  498.4 4.8 copy-start.7
  498.4 4.8 copy-start.16
  498.4 4.8 copy-start.23
  499.7 21.6 %collective-permute-start.6 = (f32[2,2,4,8,1536]{4,3,2,1,0:T(8,128)}, f32[2,2,4,8,1536]{4,3,2,1,0:T(8,128)}, u32[]{:S(2)}, u32[]{:S(2)}) collective-permute-start(f32[2,2,4,8,1536]{4,3,2,1,0:T(8,128)} %get-tuple-element.211), channel_id=1, source_target_pairs={{0,1},{2,3},{4,5},{6,7},{8,9},{10,11},{12,13},{14,15},{16,17},{18,... | collective-permute-start | bytes 2359304 | tf_op jit(solution)/shard_map/ppermute | solution.py:19
  501.9 19.4 %collective-permute-start.7 = (f32[2,2,4,8,1536]{4,3,2,1,0:T(8,128)}, f32[2,2,4,8,1536]{4,3,2,1,0:T(8,128)}, u32[]{:S(2)}, u32[]{:S(2)}) collective-permute-start(f32[2,2,4,8,1536]{4,3,2,1,0:T(8,128)} %get-tuple-element.212), channel_id=1, source_target_pairs={{1,0},{3,2},{5,4},{7,6},{9,8},{11,10},{13,12},{15,14},{17,16},{19,... | collective-permute-start | bytes 2359304 | tf_op jit(solution)/shard_map/ppermute | solution.py:20
  521.3 1.7 copy-start.24
  521.3 2.8 copy-start.12
  521.3 2.8 copy-start.17
  521.3 2.8 copy-start.19
  523.3 2.7 copy-start.25
  (3 other events, 4.0 us)
Sparse Core Ops, SparseCore 0:
  350.7 164.4 all-reduce.4
